TPU v7x, 512 devices: a whole 4x8x8 slice. The times are simulated.
512 devices in a mesh: region: 128 (over z, y, core), hour: 4 (over x).
Axes of the slice: x: 4, y: 8, z: 8, core: 2. Of those that a mesh axis runs over, the one named last changes fastest.
Arguments:
- kkt_inverse: bfloat16 [128, 1024, 1024], P('region'), may hold values from -1 to 2
- demand: float32 [512, 131072], P('hour', 'region'), may hold values from -6 to 6
- cost_quad: float32 [131072], P('region'), may hold values from 0.1 to 2
- cost_lin: float32 [131072], P('region'), may hold values from -1 to 1
- capacity: float32 [131072], P('region'), may hold values from 0.2 to 2
- ramp: float32 [131072], P('region'), may hold values from 0.05 to 1
- gen_start: float32 [131072], P('region'), may hold values from 0 to 1
- boundary_bus: int32 [128, 2, 128], P('region'), may hold values from 0 to 1023
- tie_count: int32 [128], replicated, may hold values from 32 to 128, as said below
- part_bus: int32 [1024, 8], replicated, may hold values from 0 to 131071
- part_share: float32 [1024, 8], replicated, may hold values from 0.05 to 1
- cleared_mw: float32 [4, 128, 1024], P('hour', 'region'), may hold values from -6 to 6
Outputs:
- angles: float32 [512, 131072], P('hour', 'region')
- payment: float32 [4, 128, 1024], P('hour', 'region')
Inputs may be any that keep to these rules, and one draw needn't show every extreme that they name: Tie lines pair up in order: slots below tie_count[r] of region r's right block meet the same slots of the next region's left block (the last region's next is region 0); some region has 128 live tie lines.
All inputs are finite; a program needn't handle non-finite values.
Results may differ from a plain program's by a relative error of at most 0.0062.
Values may be sent and summed in bfloat16 or wider, within the bound.
A program may use at most 64 MiB of HBM per device.

v0:
```python
import jax
import jax.numpy as jnp
from jax import lax
from jax.sharding import PartitionSpec as P

ITERS = 2


def shifted(shard, axis, by):
    length = lax.axis_size(axis)
    return lax.ppermute(shard, axis, [(i, (i + by) % length) for i in range(length)])


def from_behind(value, axis, steps):
    count = lax.axis_size(axis)
    leading, last = (max(0, -steps), min(count, count - steps))
    return lax.ppermute(value, axis, [(source, source + steps) for source in range(leading, last)])


def shards(
    kkt_inverse,
    demand,
    cost_quad,
    cost_lin,
    capacity,
    ramp,
    gen_start,
    boundary_bus,
    tie_count,
    part_bus,
    part_share,
    cleared_mw,
):
    region = lax.axis_index("region")
    region_count = lax.axis_size("region")
    block_index = lax.axis_index("hour")
    matrix = kkt_inverse[0]
    buses_here = matrix.shape[0]
    slot_count = boundary_bus.shape[2]
    slot_ids = jnp.arange(slot_count, dtype=jnp.int32)
    left_count = tie_count[(region + region_count - 1) % region_count]
    right_count = tie_count[region]
    live_mask = jnp.concatenate([slot_ids < left_count, slot_ids < right_count]).astype(jnp.float32)
    slot_bus = boundary_bus[0].reshape(-1)
    slot_table = (slot_bus[:, None] == jnp.arange(buses_here, dtype=jnp.int32)[None, :]).astype(
        jnp.float32
    )
    exact = lax.Precision.HIGHEST
    generation = jnp.zeros(demand.shape, jnp.float32)
    dual_var = jnp.zeros(demand.shape, jnp.float32)
    tie_mean = jnp.zeros((demand.shape[0], 2 * slot_count), jnp.float32)
    tie_dual = jnp.zeros((demand.shape[0], 2 * slot_count), jnp.float32)
    angles = generation
    for iteration in range(ITERS):
        tie_term = jnp.dot(
            live_mask * (tie_mean - tie_dual),
            slot_table,
            precision=exact,
            preferred_element_type=jnp.float32,
        )
        right_side = (demand + (generation - dual_var) + tie_term).astype(jnp.bfloat16)
        angles = lax.dot_general(
            right_side, matrix, (((1,), (1,)), ((), ())), preferred_element_type=jnp.float32
        )
        at_ends = lax.dot_general(
            angles,
            slot_table,
            (((1,), (1,)), ((), ())),
            precision=exact,
            preferred_element_type=jnp.float32,
        )
        tie_ends = at_ends + tie_dual
        from_left = shifted(tie_ends[:, slot_count:], "region", 1)
        from_right = shifted(tie_ends[:, :slot_count], "region", -1)
        far_ends = jnp.concatenate([from_left, from_right], axis=1)
        tie_mean = live_mask * (tie_ends + far_ends) * 0.5
        tie_dual = live_mask * (tie_dual + at_ends - tie_mean)
        edge_gen = from_behind(generation[-1:], "hour", 1)
        edge_gen = jnp.where(block_index == 0, gen_start[None, :], edge_gen)
        prior_gen = jnp.concatenate([edge_gen, generation[:-1]], axis=0)
        target = (angles + dual_var - cost_lin) / (cost_quad + 1.0)
        limited = jnp.minimum(jnp.maximum(target, prior_gen - ramp), prior_gen + ramp)
        generation = jnp.minimum(jnp.maximum(limited, 0.0), capacity)
        dual_var = dual_var + angles - generation
    prices_bf = dual_var.astype(jnp.bfloat16)
    owner_region = part_bus // buses_here
    local_bus = jnp.clip(part_bus - region * buses_here, 0, buses_here - 1)
    in_region = owner_region == region
    picked = jnp.take(prices_bf, local_bus, axis=1).astype(jnp.float32)
    partial_price = jnp.sum(jnp.where(in_region, picked * part_share, 0.0), axis=-1)
    prices = lax.psum_scatter(partial_price, "region", scatter_dimension=0, tiled=True)
    payment = cleared_mw * prices[None]
    return (angles, payment)


def solution(mesh):
    return jax.shard_map(
        shards,
        mesh=mesh,
        in_specs=(
            P("region", None, None),
            P("hour", "region"),
            P("region"),
            P("region"),
            P("region"),
            P("region"),
            P("region"),
            P("region", None, None),
            P(),
            P(),
            P(),
            P("hour", "region", None),
        ),
        out_specs=(P("hour", "region"), P("hour", "region", None)),
        check_vma=False,
    )
```

profile of v0, /device:TPU:1, one launch (start us, length us, event | category | flops | bytes accessed | tf_op | source)
XLA Modules:
  0.0 276.9 jit_solution(12809705962805588373)
XLA Ops:
  7.2 0.0 copy-start
  7.2 0.0 copy-start.6
  7.2 0.0 copy-start.2
  7.2 0.0 copy-start.3
  7.2 0.0 copy-start.7
  7.2 0.0 copy-start.8
  7.2 0.0 copy-start.9
  7.2 0.0 all-reduce.4.cloned.1.call-start
  7.3 4.1 %collective-permute-start = (f32[1,1024]{1,0:T(1,128)S(1)}, f32[1,1024]{1,0:T(1,128)S(1)}, u32[]{:S(2)}, u32[]{:S(2)}) collective-permute-start(f32[1,1024]{1,0:T(1,128)S(1)} %slice.16), channel_id=1, source_target_pairs={{0,1},{1,2},{2,3},{4,5},{5,6},{6,7},{8,9},{9,10},{10,11},{12,13},{... | collective-permute-start | bytes 12296 | tf_op jit(solution)/shard_map/ppermute | solution.py:17
  11.4 0.7 broadcast_add_fusion
  12.1 0.8 compare_and_fusion
  12.9 0.2 copy.25
  13.1 0.3 reshape.30
  13.4 1.6 fusion.4
  15.0 0.0 copy-done.6
  15.0 0.6 fusion.33
  15.6 1.3 iota_compare_fusion.4
  16.9 0.0 copy-done.2
  16.9 0.2 copy.27
  17.1 0.3 copy.23
  17.4 0.3 copy.24
  17.7 0.0 collective-permute-done
  17.7 0.0 copy-done.3
  17.7 0.0 copy-done
  17.7 0.0 copy-done.7
  17.7 0.0 copy-done.8
  17.7 0.0 copy-done.9
  17.8 0.0 copy-start.4
  17.8 0.0 copy-start.1
  17.8 0.9 fusion.10
  18.7 3.1 %collective-permute-start.3 = (f32[1,1024]{1,0:T(1,128)S(1)}, f32[1,1024]{1,0:T(1,128)S(1)}, u32[]{:S(2)}, u32[]{:S(2)}) collective-permute-start(f32[1,1024]{1,0:T(1,128)S(1)} %slice.25), channel_id=1, source_target_pairs={{0,1},{1,2},{2,3},{4,5},{5,6},{6,7},{8,9},{9,10},{10,11},{12,13},{... | collective-permute-start | bytes 12296 | tf_op jit(solution)/shard_map/ppermute | solution.py:17
  21.8 0.0 copy-done.4
  21.8 0.8 fusion.6
  22.6 4.3 %collective-permute-start.2 = (f32[128,128]{1,0:T(8,128)S(1)}, f32[128,128]{1,0:T(8,128)S(1)}, u32[]{:S(2)}, u32[]{:S(2)}) collective-permute-start(f32[128,128]{1,0:T(8,128)S(1)} %get-tuple-element.5), channel_id=1, source_target_pairs={{0,508},{4,0},{8,4},{12,8},{16,12},{20,16},{24,20},{28,24},{32,28}... | collective-permute-start | bytes 196616 | tf_op jit(solution)/shard_map/ppermute | solution.py:11
  26.9 2.0 collective-permute-start.1
  28.9 0.0 collective-permute-done.3
  28.9 0.0 collective-permute-done.2
  28.9 10.3 %collective-permute-done.1 = f32[128,128]{1,0:T(8,128)S(1)} collective-permute-done((f32[128,128]{1,0:T(8,128)S(1)}, f32[128,128]{1,0:T(8,128)S(1)}, u32[]{:S(2)}, u32[]{:S(2)}) %collective-permute-start.1) | collective-permute-done | bytes 65568 | tf_op jit(solution)/shard_map/ppermute | solution.py:11
  39.2 0.0 copy-done.1
  39.2 0.7 fusion.5
  40.0 1.7 subtract_convert_fusion
  41.7 0.2 copy.26
  41.9 29.2 %gather_fusion = bf16[8192,128]{1,0:T(8,128)(2,1)} fusion(bf16[128,1024]{0,1:T(8,128)(2,1)S(1)} %copy.26, s32[8192]{0:T(1024)S(1)} %broadcast_clamp_fusion), kind=kCustom, calls=%fused_computation | custom fusion | bytes 4227072 | tf_op jit(solution)/shard_map/jit(_take)/gather | solution.py:89
  71.1 0.0 copy-start.5
  71.2 7.1 %select_reduce_fusion = f32[1024,128]{1,0:T(8,128)S(1)} fusion(bf16[8192,128]{1,0:T(8,128)(2,1)} %gather_fusion, f32[1024,8]{1,0:T(8,128)S(1)} %copy.27, pred[1024,8]{1,0:T(8,128)(4,1)S(1)} %copy.23, pred[1024,8]{1,0:T(8,128)(4,1)S(1)} %copy.24), kind=kLoop, calls=%fused_computation.1 | loop fusion | flops 5111808 | bytes 2670592 | tf_op jit(solution)/shard_map/reduce_sum | solution.py:90
  78.3 1.0 copy.28
  79.3 0.0 all-reduce.4.cloned.1.call-update
  79.3 1.3 dynamic-slice
  80.6 187.4 %all-reduce.4.cloned.1.call-done = f32[128,1024]{1,0:T(8,128)} async-done(((f32[128,1024]{1,0:T(8,128)}), f32[128,1024]{1,0:T(8,128)}) %all-reduce.4.cloned.1.call-update) | async-done | bytes 524304
  268.1 0.0 copy-done.5
  268.1 2.0 fusion.27
  (7 shorter events, 0.1 us)
Async XLA Ops:
  7.2 10.6 %copy-start = (bf16[1,1024,1024]{2,1,0:T(8,128)(2,1)S(1)}, bf16[1,1024,1024]{2,1,0:T(8,128)(2,1)}, u32[]{:S(2)}) copy-start(bf16[1,1024,1024]{2,1,0:T(8,128)(2,1)} %param.12) | copy-start | bytes 6291460
  7.2 7.8 %copy-start.6 = (s32[128]{0:T(128)S(1)}, s32[128]{0:T(128)}, u32[]{:S(2)}) copy-start(s32[128]{0:T(128)} %param.20) | copy-start | bytes 1540
  7.2 9.7 %copy-start.2 = (f32[1024,8]{0,1:T(8,128)S(1)}, f32[1024,8]{0,1:T(8,128)}, u32[]{:S(2)}) copy-start(f32[1024,8]{0,1:T(8,128)} %param.22) | copy-start | bytes 98308
  7.2 10.5 %copy-start.3 = (f32[1024]{0:T(1024)S(1)}, f32[1024]{0:T(1024)}, u32[]{:S(2)}) copy-start(f32[1024]{0:T(1024)} %param.18) | copy-start | bytes 12292
  7.2 10.5 %copy-start.7 = (f32[1024]{0:T(1024)S(1)}, f32[1024]{0:T(1024)}, u32[]{:S(2)}) copy-start(f32[1024]{0:T(1024)} %param.16) | copy-start | bytes 12292
  7.2 10.5 %copy-start.8 = (f32[1024]{0:T(1024)S(1)}, f32[1024]{0:T(1024)}, u32[]{:S(2)}) copy-start(f32[1024]{0:T(1024)} %param.17) | copy-start | bytes 12292
  7.2 10.5 %copy-start.9 = (f32[1024]{0:T(1024)S(1)}, f32[1024]{0:T(1024)}, u32[]{:S(2)}) copy-start(f32[1024]{0:T(1024)} %param.15) | copy-start | bytes 12292
  7.2 260.8 %all-reduce.4.cloned.1.call-start = ((), (), s32[]{:S(2)}) async-start(), calls=%async_computation | async-start | bytes 1048576
  7.3 10.4 %collective-permute-start = (f32[1,1024]{1,0:T(1,128)S(1)}, f32[1,1024]{1,0:T(1,128)S(1)}, u32[]{:S(2)}, u32[]{:S(2)}) collective-permute-start(f32[1,1024]{1,0:T(1,128)S(1)} %slice.16), channel_id=1, source_target_pairs={{0,1},{1,2},{2,3},{4,5},{5,6},{6,7},{8,9},{9,10},{10,11},{12,13},{... | collective-permute-start | bytes 12296 | tf_op jit(solution)/shard_map/ppermute | solution.py:17
  17.8 4.1 %copy-start.4 = (s32[1,2,128]{2,1,0:T(2,128)S(1)}, s32[1,2,128]{2,1,0:T(2,128)}, u32[]{:S(2)}) copy-start(s32[1,2,128]{2,1,0:T(2,128)} %param.19) | copy-start | bytes 3076
  17.8 21.5 %copy-start.1 = (f32[128,1024]{1,0:T(8,128)S(1)}, f32[128,1024]{1,0:T(8,128)}, u32[]{:S(2)}) copy-start(f32[128,1024]{1,0:T(8,128)} %param.13) | copy-start | bytes 1572868
  18.7 10.2 %collective-permute-start.3 = (f32[1,1024]{1,0:T(1,128)S(1)}, f32[1,1024]{1,0:T(1,128)S(1)}, u32[]{:S(2)}, u32[]{:S(2)}) collective-permute-start(f32[1,1024]{1,0:T(1,128)S(1)} %slice.25), channel_id=1, source_target_pairs={{0,1},{1,2},{2,3},{4,5},{5,6},{6,7},{8,9},{9,10},{10,11},{12,13},{... | collective-permute-start | bytes 12296 | tf_op jit(solution)/shard_map/ppermute | solution.py:17
  22.6 6.3 %collective-permute-start.2 = (f32[128,128]{1,0:T(8,128)S(1)}, f32[128,128]{1,0:T(8,128)S(1)}, u32[]{:S(2)}, u32[]{:S(2)}) collective-permute-start(f32[128,128]{1,0:T(8,128)S(1)} %get-tuple-element.5), channel_id=1, source_target_pairs={{0,508},{4,0},{8,4},{12,8},{16,12},{20,16},{24,20},{28,24},{32,28}... | collective-permute-start | bytes 196616 | tf_op jit(solution)/shard_map/ppermute | solution.py:11
  26.9 12.3 %collective-permute-start.1 = (f32[128,128]{1,0:T(8,128)S(1)}, f32[128,128]{1,0:T(8,128)S(1)}, u32[]{:S(2)}, u32[]{:S(2)}) collective-permute-start(f32[128,128]{1,0:T(8,128)S(1)} %get-tuple-element.4), channel_id=1, source_target_pairs={{0,4},{4,8},{8,12},{12,16},{16,20},{20,24},{24,28},{28,32},{32,36}... | collective-permute-start | bytes 196616 | tf_op jit(solution)/shard_map/ppermute | solution.py:11
  71.1 196.9 %copy-start.5 = (f32[1,1,1024]{2,1,0:T(1,128)S(1)}, f32[1,1,1024]{2,1,0:T(1,128)}, u32[]{:S(2)}) copy-start(f32[1,1,1024]{2,1,0:T(1,128)} %param.23) | copy-start | bytes 12292
Sparse Core Ops, SparseCore 0:
  79.4 188.5 all-reduce.3
where the time goes:
time: 278 us; the launch traced here: 277 us
  waiting for transfers between devices  198 us (71%)
  local copies, waits for them, and re-layouts  33.6 us (12%)
  between operations  14.4 us (5%)
  starting transfers between devices  13.5 us (5%)
  other arithmetic  12 us (4%)
  matrix products  5.76 us (2%)
    unnamed x2, waiting for transfers between devices  187 us
    gather x1, local copies, waits for them, and re-layouts, shards(): picked = jnp.take(prices_bf, local_bus, axis=1).astype(jnp.float32)  29.2 us
    ppermute x2, waiting for transfers between devices, shifted(): lax.ppermute(shard, axis, [(i, (i + by) % length) for i in range(length)])  10.3 us
    ppermute x2, starting transfers between devices, from_behind(): lax.ppermute(value, axis, [(source, source + steps) for source in range(l...  7.19 us
    reduce_sum x1, other arithmetic, shards(): jnp.sum(jnp.where(in_region, picked * part_share, 0.0), axis=-1)  7.1 us
    ppermute x2, starting transfers between devices, shifted(): lax.ppermute(shard, axis, [(i, (i + by) % length) for i in range(length)])  6.24 us
  transfers between devices with their start and end apart: 5, of which 2 were waited for; matrix products, arithmetic and copies ran while one was open for 3% of the time, Pallas kernels for 0%

commit v1 on v0

v1 whole, which is shorter than its diff:
```python
import functools

import jax
import jax.numpy as jnp
from jax import lax
from jax.experimental import pallas as pl
from jax.experimental.pallas import tpu as pltpu
from jax.sharding import PartitionSpec as P

MESH = pl.DeviceIdType.MESH
NT = (((1,), (1,)), ((), ()))
LANES = 128


def spread(step, size):
    return (size // 2 + (1 - 2 * (step % 2)) * ((step + 1) // 2)) % size


def kernel(
    torus,
    tie_count,
    kkt_hbm,
    demand_hbm,
    cost_quad,
    cost_lin,
    capacity,
    ramp,
    gen_start,
    boundary,
    part_bus,
    part_share,
    cleared,
    angles_ref,
    payment_ref,
    kkt,
    demand,
    rhs,
    base,
    dual,
    gen,
    slots,
    shares,
    tie_out,
    tie_in,
    edge_out,
    edge_in,
    stage,
    outbox,
    inbox,
    kkt_sem,
    demand_sem,
    tie_send,
    tie_recv,
    edge_send,
    edge_recv,
    price_send,
    price_recv,
):
    size_z, size_y, size_c = torus
    regions = size_z * size_y * size_c
    region = lax.axis_index("region")
    block = lax.axis_index("hour")
    blocks = lax.axis_size("hour")
    right = (region + 1) % regions
    left = (region + regions - 1) % regions
    later = (block + 1) % blocks
    earlier = (block + blocks - 1) % blocks
    hours, buses = demand.shape
    tie_slots = boundary.shape[1]
    chunk = min(256, buses)
    chunks = buses // chunk
    parts = part_bus.shape[1]
    taps = part_bus.shape[0]

    kkt_copies = [
        pltpu.make_async_copy(
            kkt_hbm.at[0, pl.ds(c * chunk, chunk)], kkt.at[pl.ds(c * chunk, chunk)], kkt_sem.at[c]
        )
        for c in range(chunks)
    ]
    demand_copy = pltpu.make_async_copy(demand_hbm, demand, demand_sem)
    demand_copy.start()
    for copy in kkt_copies:
        copy.start()

    barrier = pltpu.get_barrier_semaphore()

    def greet(step, carry):
        pl.semaphore_signal(
            barrier, inc=1, device_id={"region": (region + step) % regions}, device_id_type=MESH
        )
        return carry

    lax.fori_loop(1, regions, greet, 0)
    for neighbour in (earlier, later):
        pl.semaphore_signal(barrier, inc=1, device_id={"hour": neighbour}, device_id_type=MESH)

    lane = lax.broadcasted_iota(jnp.int32, (1, tie_slots), 1)
    row = lax.broadcasted_iota(jnp.int32, (chunk, tie_slots), 0)
    for side, count in ((0, tie_count[left]), (1, tie_count[region])):
        bus = jnp.where(lane < count, boundary[pl.ds(side, 1), :], -1)
        for c in range(chunks):
            slots[pl.ds(c * chunk, chunk), pl.ds(side * tie_slots, tie_slots)] = jnp.where(
                row + c * chunk == bus, 1.0, 0.0
            ).astype(jnp.bfloat16)

    scale = 1.0 / (cost_quad[...] + 1.0)

    demand_copy.wait()
    rhs[...] = demand[...].astype(jnp.bfloat16)

    first_row = lax.broadcasted_iota(jnp.int32, (hours, 1), 0) == 0
    start_row = first_row & (block == 0)
    for c in range(chunks):
        cols = pl.ds(c * chunk, chunk)
        kkt_copies[c].wait()
        angles = lax.dot_general(rhs[...], kkt[cols, :], NT, preferred_element_type=jnp.float32)
        ends = jnp.dot(
            angles.astype(jnp.bfloat16), slots[cols, :], preferred_element_type=jnp.float32
        )
        if c == 0:
            stage_ends = ends
        else:
            stage_ends = stage_ends + ends
        prior = jnp.where(start_row, gen_start[:, cols], 0.0)
        target = (angles - cost_lin[:, cols]) * scale[:, c * chunk : (c + 1) * chunk]
        limited = jnp.minimum(jnp.maximum(target, prior - ramp[:, cols]), prior + ramp[:, cols])
        made = jnp.minimum(jnp.maximum(limited, 0.0), capacity[:, cols])
        owed = angles - made
        gen[:, cols] = made
        dual[:, cols] = owed
        base[:, cols] = demand[:, cols] + (made - owed)
        edge_out[:, cols] = made[hours - 1 :, :]
    for side in range(2):
        tie_out[side] = stage_ends[:, side * tie_slots : (side + 1) * tie_slots].astype(jnp.bfloat16)

    rows = min(64, buses)
    bus_row = lax.broadcasted_iota(jnp.int32, (rows, LANES), 0)

    def fill(step, carry):
        start = step * rows
        for j in range(parts // LANES):
            cols = pl.ds(j * LANES, LANES)
            total = jnp.zeros((rows, LANES), jnp.float32)
            for k in range(taps):
                here = part_bus[pl.ds(k, 1), cols] - (region * buses + start)
                total = total + jnp.where(bus_row == here, part_share[pl.ds(k, 1), cols], 0.0)
            shares[pl.ds(pl.multiple_of(start, rows), rows), cols] = total.astype(jnp.bfloat16)
        return carry

    half = (buses // rows) // 2
    lax.fori_loop(0, half, fill, 0)

    pl.semaphore_wait(barrier, regions + 1)

    ties = [
        pltpu.make_async_remote_copy(
            src_ref=tie_out.at[1 - side],
            dst_ref=tie_in.at[side],
            send_sem=tie_send.at[side],
            recv_sem=tie_recv.at[side],
            device_id={"region": to},
            device_id_type=MESH,
        )
        for side, to in ((0, right), (1, left))
    ]
    edge = pltpu.make_async_remote_copy(
        src_ref=edge_out,
        dst_ref=edge_in,
        send_sem=edge_send,
        recv_sem=edge_recv,
        device_id={"hour": later},
        device_id_type=MESH,
    )
    for copy in ties:
        copy.start()
    edge.start()

    lax.fori_loop(half, buses // rows, fill, 0)

    for copy in ties:
        copy.wait()
    edge.wait()

    for c in range(chunks):
        cols = pl.ds(c * chunk, chunk)
        tied = base[:, cols]
        for side in range(2):
            tied = tied + lax.dot_general(
                tie_in[side],
                slots[cols, pl.ds(side * tie_slots, tie_slots)],
                NT,
                preferred_element_type=jnp.float32,
            )
        rhs[:, cols] = tied.astype(jnp.bfloat16)

    for c in range(chunks):
        cols = pl.ds(c * chunk, chunk)
        angles = lax.dot_general(rhs[...], kkt[cols, :], NT, preferred_element_type=jnp.float32)
        angles_ref[:, cols] = angles
        before = jnp.where(block == 0, gen_start[:, cols], edge_in[:, cols])
        prior = jnp.where(first_row, before, pltpu.roll(gen[:, cols], 1, 0))
        owed = dual[:, cols]
        target = (angles + owed - cost_lin[:, cols]) * scale[:, c * chunk : (c + 1) * chunk]
        limited = jnp.minimum(jnp.maximum(target, prior - ramp[:, cols]), prior + ramp[:, cols])
        made = jnp.minimum(jnp.maximum(limited, 0.0), capacity[:, cols])
        base[:, cols] = owed + angles - made

    lmp = base[...].astype(jnp.bfloat16)
    pieces = parts // LANES
    width = min(256, parts)
    for c in range(parts // width):
        part = jnp.dot(lmp, shares[:, pl.ds(c * width, width)], preferred_element_type=jnp.float32)
        for i in range(width // LANES):
            stage[pl.ds(c * (width // LANES) + i, hours, stride=pieces), :] = part[
                :, i * LANES : (i + 1) * LANES
            ]
    outbox[...] = stage[...].reshape(hours, pieces, LANES).astype(jnp.bfloat16)

    here_z = region // (size_y * size_c)
    here_y = (region // size_c) % size_y
    here_c = region % size_c

    def send(to):
        pltpu.make_async_remote_copy(
            src_ref=outbox.at[to],
            dst_ref=inbox.at[region],
            send_sem=price_send,
            recv_sem=price_recv,
            device_id={"region": to},
            device_id_type=MESH,
        ).start()

    def post(step, carry):
        to_z = (here_z + spread(step // size_y, size_z)) % size_z
        to_y = (here_y + spread(step % size_y, size_y)) % size_y
        for shift in range(size_c):
            send((to_z * size_y + to_y) * size_c + (here_c + shift) % size_c)
        return carry

    lax.fori_loop(0, size_z * size_y - 1, post, 0)
    for shift in range(1, size_c):
        send((here_z * size_y + here_y) * size_c + (here_c + shift) % size_c)
    inbox[region] = outbox[region]

    others = pl.ds(0, regions - 1)
    whole = pltpu.make_async_remote_copy(
        src_ref=outbox.at[others],
        dst_ref=inbox.at[others],
        send_sem=price_send,
        recv_sem=price_recv,
        device_id={"region": right},
        device_id_type=MESH,
    )
    whole.wait_recv()
    price = jnp.sum(inbox[...].astype(jnp.float32), axis=0)
    payment_ref[...] = cleared[...] * price
    whole.wait_send()


def settle(torus, *operands):
    (
        kkt_inverse,
        demand,
        cost_quad,
        cost_lin,
        capacity,
        ramp,
        gen_start,
        boundary_bus,
        tie_count,
        part_bus,
        part_share,
        cleared_mw,
    ) = operands
    hours, buses = demand.shape
    tie_slots = boundary_bus.shape[2]
    parts = part_bus.shape[0]
    pieces = parts // LANES
    regions = torus[0] * torus[1] * torus[2]
    chunks = max(1, buses // 256)
    line = lambda value: value.reshape(1, buses)
    vmem = pl.BlockSpec(memory_space=pltpu.VMEM)
    hbm = pl.BlockSpec(memory_space=pl.ANY)
    bf16, f32 = jnp.bfloat16, jnp.float32
    angles, payment = pl.pallas_call(
        functools.partial(kernel, torus),
        out_shape=(
            jax.ShapeDtypeStruct((hours, buses), f32),
            jax.ShapeDtypeStruct((pieces, LANES), f32),
        ),
        in_specs=[pl.BlockSpec(memory_space=pltpu.SMEM), hbm, hbm] + [vmem] * 9,
        out_specs=(vmem, vmem),
        scratch_shapes=[
            pltpu.VMEM((buses, buses), bf16),
            pltpu.VMEM((hours, buses), f32),
            pltpu.VMEM((hours, buses), bf16),
            pltpu.VMEM((hours, buses), f32),
            pltpu.VMEM((hours, buses), f32),
            pltpu.VMEM((hours, buses), f32),
            pltpu.VMEM((buses, 2 * tie_slots), bf16),
            pltpu.VMEM((buses, parts), bf16),
            pltpu.VMEM((2, hours, tie_slots), bf16),
            pltpu.VMEM((2, hours, tie_slots), bf16),
            pltpu.VMEM((1, buses), f32),
            pltpu.VMEM((1, buses), f32),
            pltpu.VMEM((hours * pieces, LANES), f32),
            pltpu.VMEM((regions, pieces, LANES), bf16),
            pltpu.VMEM((regions, pieces, LANES), bf16),
            pltpu.SemaphoreType.DMA((chunks,)),
            pltpu.SemaphoreType.DMA,
            pltpu.SemaphoreType.DMA((2,)),
            pltpu.SemaphoreType.DMA((2,)),
            pltpu.SemaphoreType.DMA,
            pltpu.SemaphoreType.DMA,
            pltpu.SemaphoreType.DMA,
            pltpu.SemaphoreType.DMA,
        ],
        compiler_params=pltpu.CompilerParams(collective_id=0, has_side_effects=True),
    )(
        tie_count,
        kkt_inverse,
        demand,
        line(cost_quad),
        line(cost_lin),
        line(capacity),
        line(ramp),
        line(gen_start),
        boundary_bus[0],
        part_bus.T,
        part_share.T,
        cleared_mw.reshape(pieces, LANES),
    )
    return angles, payment.reshape(cleared_mw.shape)


def solution(mesh, torus=(8, 8, 2)):
    return jax.shard_map(
        functools.partial(settle, torus),
        mesh=mesh,
        in_specs=(
            P("region", None, None),
            P("hour", "region"),
            P("region"),
            P("region"),
            P("region"),
            P("region"),
            P("region"),
            P("region", None, None),
            P(),
            P(),
            P(),
            P("hour", "region", None),
        ),
        out_specs=(P("hour", "region"), P("hour", "region", None)),
        check_vma=False,
    )
```

time: 278 us -> 39.1 us (0.14)
  waiting for transfers between devices: 198 us -> 0 us
  Pallas kernels: 0 us -> 35 us
  local copies, waits for them, and re-layouts: 33.6 us -> 3.15 us
  between operations: 14.4 us -> 0.64 us
  starting transfers between devices: 13.5 us -> 0 us
  other arithmetic: 12 us -> 0 us
  matrix products: 5.76 us -> 0 us
    unnamed x2 -> x0, waiting for transfers between devices: 187 us -> none
    pallas_call x0 -> x1, Pallas kernels: none -> 35 us  [settle(): pl.pallas_call(functools.partial(kernel, torus), out_shape=(jax.ShapeDtyp...]
    gather x1 -> x0, local copies, waits for them, and re-layouts: 29.2 us -> none  [shards(): picked = jnp.take(prices_bf, local_bus, axis=1).astype(jnp.float32)]
    ppermute x4 -> x0, starting transfers between devices: 13.4 us -> none  [the longest x2 7.19 us: from_behind(): lax.ppermute(value, axis, [(source, source + steps) for source in range(l...]
    ppermute x4 -> x0, waiting for transfers between devices: 10.3 us -> none  [the longest x2 10.3 us: shifted(): lax.ppermute(shard, axis, [(i, (i + by) % length) for i in range(length)])]
    reduce_sum x1 -> x0, other arithmetic: 7.1 us -> none  [shards(): jnp.sum(jnp.where(in_region, picked * part_share, 0.0), axis=-1)]
    dot_general x5 -> x0, matrix products: 5.76 us -> none  [the longest x2 2.61 us: shards(): lax.dot_general(right_side, matrix, (((1,), (1,)), ((), ())), preferred_e...]
  transfers between devices with their start and end apart: 5 -> 0, of which waited for: 2 -> 0; matrix products, arithmetic and copies ran while one was open for 3% -> 0% of each run, Pallas kernels for 0% -> 0%
where the time goes in v1:
time: 39.1 us; the launch traced here: 38.8 us
  Pallas kernels  35 us (90%)
  local copies, waits for them, and re-layouts  3.15 us (8%)
  between operations  0.64 us (2%)
    pallas_call x1, Pallas kernels, settle(): pl.pallas_call(functools.partial(kernel, torus), out_shape=(jax.ShapeDtyp...  35 us
    unnamed x2, local copies, waits for them, and re-layouts  3.15 us

profile of v1, /device:TPU:1, one launch (start us, length us, event | category | flops | bytes accessed | tf_op | source)
XLA Modules:
  0.0 38.8 jit_solution(11458737894160292840)
XLA Ops:
  0.6 35.0 %shard_map.131 = (f32[128,1024]{1,0:T(8,128)}, f32[8,128]{1,0:T(8,128)}) custom-call(s32[128]{0:T(128)} %tie_count.1, bf16[1,1024,1024]{2,1,0:T(8,128)(2,1)} %kkt_hbm.1, f32[128,1024]{1,0:T(8,128)} %demand_hbm.1, f32[1,1024]{1,0:T(1,128)} %bitcast.12, f32[1,1024]{1,0:T(1,128)} %bitcast.13, f32[1,1024]{1,0:T(1,128)} %bitcast.14, f32[1,1024]{1,0:T(1,128)} %bitcast.15, ...), custom_call_target="tpu_custom_call" | custom-call | tf_op jit(solution)/shard_map/pallas_call | solution.py:286
  35.6 1.9 %copy.16 = f32[128,1024]{1,0:T(8,128)} copy(f32[128,1024]{1,0:T(8,128)} %get-tuple-element.8) | data formatting | bytes 1048576
  37.5 1.3 %copy.17 = f32[1,1,1024]{2,1,0:T(1,128)} copy(f32[1,1,1024]{2,1,0:T(1,128)} %bitcast.18) | data formatting | bytes 8192

commit v2 on v1

v2 whole, which is shorter than its diff:
```python
import functools

import jax
import jax.numpy as jnp
from jax import lax
from jax.experimental import pallas as pl
from jax.experimental.pallas import tpu as pltpu
from jax.sharding import PartitionSpec as P

MESH = pl.DeviceIdType.MESH
NT = (((1,), (1,)), ((), ()))
LANES = 128
PAD = 8


def far_first(size):
    return sorted(range(1, size), key=lambda shift: -min(shift, size - shift))


def kernel(
    torus,
    boundary_hbm,
    tie_count_hbm,
    demand_hbm,
    kkt_hbm,
    cost_quad_hbm,
    cost_lin_hbm,
    capacity_hbm,
    ramp_hbm,
    gen_start_hbm,
    part_bus_hbm,
    part_share_hbm,
    angles_ref,
    price_ref,
    boundary,
    tie_count,
    demand,
    kkt,
    cost_quad,
    cost_lin,
    capacity,
    ramp,
    gen_start,
    part_bus,
    part_share,
    rhs,
    lmp,
    base,
    dual,
    gen,
    slots,
    spread,
    shares,
    tie_out,
    tie_in,
    edge_out,
    edge_in,
    stage,
    out_y,
    out_z,
    in_y,
    in_z,
    out_last,
    in_last,
    load_sem,
    kkt_sem,
    tie_send,
    tie_recv,
    edge_sem,
    ring_send,
    ring_recv,
    last_sem,
):
    size_z, size_y, size_c = torus
    regions = size_z * size_y * size_c
    region = lax.axis_index("region")
    block = lax.axis_index("hour")
    blocks = lax.axis_size("hour")
    z = region // (size_y * size_c)
    y = (region // size_c) % size_y
    core = region % size_c
    right = (region + 1) % regions
    left = (region + regions - 1) % regions
    later = (block + 1) % blocks
    earlier = (block + blocks - 1) % blocks
    hours, buses = demand.shape
    tie_slots = boundary.shape[1]
    chunk = min(256, buses)
    chunks = buses // chunk
    taps, parts = part_bus.shape
    pieces = parts // LANES
    f32, bf16 = jnp.float32, jnp.bfloat16

    def at(to_z, to_y, to_c):
        return {"region": (to_z * size_y + to_y) * size_c + to_c}

    def load(index, source, target):
        copy = pltpu.make_async_copy(source, target, load_sem.at[index])
        copy.start()
        return copy

    def send(source, target, sems, to):
        copy = pltpu.make_async_remote_copy(
            src_ref=source,
            dst_ref=target,
            send_sem=sems[0],
            recv_sem=sems[1],
            device_id=to,
            device_id_type=MESH,
        )
        copy.start()
        return copy

    slot_loads = [load(0, boundary_hbm, boundary), load(1, tie_count_hbm, tie_count)]
    demand_load = load(2, demand_hbm, demand)
    kkt_loads = []
    for c in range(chunks):
        copy = pltpu.make_async_copy(
            kkt_hbm.at[0, pl.ds(c * chunk, chunk)], kkt.at[pl.ds(c * chunk, chunk)], kkt_sem.at[c]
        )
        copy.start()
        kkt_loads.append(copy)
    cost_loads = [
        load(3, cost_quad_hbm, cost_quad),
        load(4, cost_lin_hbm, cost_lin),
        load(5, capacity_hbm, capacity),
        load(6, ramp_hbm, ramp),
        load(7, gen_start_hbm, gen_start),
    ]
    part_loads = [load(8, part_bus_hbm, part_bus), load(9, part_share_hbm, part_share)]

    barrier = pltpu.get_barrier_semaphore()
    shifts_y = far_first(size_y)
    shifts_z = far_first(size_z)
    greeted = 0

    def greet(to):
        pl.semaphore_signal(barrier, inc=1, device_id=to, device_id_type=MESH)
        return 1

    for shift in shifts_y:
        for other in range(size_c):
            greeted += greet(at(z, (y + shift) % size_y, (core + other) % size_c))
    for shift in shifts_z:
        for other in range(size_c):
            greeted += greet(at((z + shift) % size_z, y, (core + other) % size_c))
    greeted += greet(at(z, y, 1 - core))
    for neighbour in (right, left):
        greeted += greet({"region": neighbour})
    for neighbour in (earlier, later):
        greeted += greet({"hour": neighbour})

    for copy in slot_loads:
        copy.wait()
    lane = lax.broadcasted_iota(jnp.int32, (1, tie_slots), 1)
    owner = lax.broadcasted_iota(jnp.int32, (1, regions), 1)
    row = lax.broadcasted_iota(jnp.int32, (chunk, tie_slots), 0)
    for side, edge_region in ((0, left), (1, region)):
        count = jnp.sum(
            jnp.where(owner == edge_region, tie_count[...], 0), axis=1, keepdims=True
        )
        bus = jnp.where(lane < count, boundary[pl.ds(side, 1), :], -1)
        for c in range(chunks):
            slots[pl.ds(c * chunk, chunk), pl.ds(side * tie_slots, tie_slots)] = jnp.where(
                row + c * chunk == bus, 1.0, 0.0
            ).astype(bf16)

    demand_load.wait()
    rhs[...] = demand[...].astype(bf16)
    for c in range(chunks):
        cols = pl.ds(c * chunk, chunk)
        kkt_loads[c].wait()
        angles = lax.dot_general(rhs[...], kkt[cols, :], NT, preferred_element_type=f32)
        angles_ref[:, cols] = angles
        part = jnp.dot(angles.astype(bf16), slots[cols, :], preferred_element_type=f32)
        ends = part if c == 0 else ends + part
    for side in range(2):
        tie_out[side] = ends[:, side * tie_slots : (side + 1) * tie_slots].astype(bf16)

    pl.semaphore_wait(barrier, greeted)
    ties = [
        send(tie_out.at[1 - side], tie_in.at[side], (tie_send.at[side], tie_recv.at[side]), to)
        for side, to in ((0, {"region": right}), (1, {"region": left}))
    ]

    for copy in cost_loads:
        copy.wait()
    tall = min(32, hours)
    start_row = (lax.broadcasted_iota(jnp.int32, (tall, chunk), 0) == 0) & (block == 0)
    for c in range(chunks):
        cols = pl.ds(c * chunk, chunk)
        scale = 1.0 / (cost_quad[:, cols] + 1.0)
        for r in range(hours // tall):
            rows = pl.ds(r * tall, tall)
            angles = angles_ref[rows, cols]
            target = (angles - cost_lin[:, cols]) * scale
            if r == 0:
                prior = jnp.where(start_row, gen_start[:, cols], 0.0)
                limited = jnp.minimum(
                    jnp.maximum(target, prior - ramp[:, cols]), prior + ramp[:, cols]
                )
            else:
                limited = jnp.minimum(jnp.maximum(target, -ramp[:, cols]), ramp[:, cols])
            made = jnp.minimum(jnp.maximum(limited, 0.0), capacity[:, cols])
            owed = angles - made
            gen[pl.ds(PAD + r * tall, tall), cols] = made
            dual[rows, cols] = owed
            base[rows, cols] = demand[rows, cols] + (made - owed)
        edge_out[:, cols] = made[tall - 1 :, :]
    edge = send(edge_out, edge_in, (edge_sem.at[0], edge_sem.at[1]), {"hour": later})

    for copy in part_loads:
        copy.wait()
    high = buses // LANES
    tile = lax.broadcasted_iota(jnp.int32, (16, LANES), 0)

    def fill(step, carry):
        cols = pl.ds(pl.multiple_of(step * LANES, LANES), LANES)
        low = []
        for k in range(taps):
            local = part_bus[pl.ds(k, 1), cols] - region * buses
            share = part_share[pl.ds(k, 1), cols]
            low.append(jnp.broadcast_to(local & (LANES - 1), (16, LANES)))
            for i in range(high):
                held = jnp.where((local >> 7) == i, share, 0.0)
                spread[k * high + i] = jnp.broadcast_to(held, (16, LANES)).astype(bf16)
        for t in range(LANES // 16):
            ones = [jnp.where(tile + 16 * t == low[k], 1.0, 0.0).astype(bf16) for k in range(taps)]
            for i in range(high):
                total = ones[0] * spread[i]
                for k in range(1, taps):
                    total = total + ones[k] * spread[k * high + i]
                shares[pl.ds(i * LANES + t * 16, 16), cols] = total
        return carry

    lax.fori_loop(0, pieces, fill, 0)

    for copy in ties:
        copy.wait()
    for c in range(chunks):
        cols = pl.ds(c * chunk, chunk)
        tied = base[:, cols]
        for side in range(2):
            tied = tied + lax.dot_general(
                tie_in[side],
                slots[cols, pl.ds(side * tie_slots, tie_slots)],
                NT,
                preferred_element_type=f32,
            )
        rhs[:, cols] = tied.astype(bf16)

    edge.wait()
    gen[pl.ds(PAD - 1, 1), :] = jnp.where(block == 0, gen_start[...], edge_in[...])
    for c in range(chunks):
        cols = pl.ds(c * chunk, chunk)
        angles_ref[:, cols] = lax.dot_general(
            rhs[...], kkt[cols, :], NT, preferred_element_type=f32
        )
    for c in range(chunks):
        cols = pl.ds(c * chunk, chunk)
        scale = 1.0 / (cost_quad[:, cols] + 1.0)
        for r in range(hours // tall):
            rows = pl.ds(r * tall, tall)
            owed = dual[rows, cols] + angles_ref[rows, cols]
            prior = gen[pl.ds(PAD - 1 + r * tall, tall), cols]
            target = (owed - cost_lin[:, cols]) * scale
            limited = jnp.minimum(
                jnp.maximum(target, prior - ramp[:, cols]), prior + ramp[:, cols]
            )
            made = jnp.minimum(jnp.maximum(limited, 0.0), capacity[:, cols])
            lmp[rows, cols] = (owed - made).astype(bf16)

    width = min(256, parts)
    for c in range(parts // width):
        part = jnp.dot(lmp[...], shares[:, pl.ds(c * width, width)], preferred_element_type=f32)
        for i in range(width // LANES):
            stage[pl.ds(c * (width // LANES) + i, hours, stride=pieces), :] = part[
                :, i * LANES : (i + 1) * LANES
            ]
    for hour in range(hours):
        to_z, to_y, to_c = hour // (size_y * size_c), (hour // size_c) % size_y, hour % size_c
        row_price = stage[pl.ds(hour * pieces, pieces), :].astype(bf16)
        if to_c == 0:
            out_y[to_y, to_z] = row_price
        else:
            out_z[to_z, to_y] = row_price

    sems_y = (ring_send.at[0], ring_recv.at[0])
    sems_z = (ring_send.at[1], ring_recv.at[1])
    for shift_y, shift_z in zip(shifts_y, shifts_z):
        to_y, to_z = (y + shift_y) % size_y, (z + shift_z) % size_z
        send(out_y.at[to_y], in_y.at[y], sems_y, at(z, to_y, core))
        send(out_z.at[to_z], in_z.at[z], sems_z, at(to_z, y, core))

    def whole(source, target, count, sems):
        some = pl.ds(0, count)
        return pltpu.make_async_remote_copy(
            src_ref=source.at[some],
            dst_ref=target.at[some],
            send_sem=sems[0],
            recv_sem=sems[1],
            device_id={"region": right},
            device_id_type=MESH,
        )

    all_y = whole(out_y, in_y, size_y - 1, sems_y)
    all_z = whole(out_z, in_z, size_z - 1, sems_z)
    all_y.wait_recv()
    total = out_y[y].astype(f32)
    for shift in range(1, size_y):
        total = total + in_y[(y + shift) % size_y].astype(f32)
    out_last[pl.ds(0, size_z)] = total
    sems_last = (last_sem.at[0], last_sem.at[1])
    for shift in shifts_z:
        to_z = (z + shift) % size_z
        send(out_last.at[to_z], in_last.at[z * size_c + core], sems_last, at(to_z, y, 0))
    all_z.wait_recv()
    total = out_z[z].astype(f32)
    for shift in range(1, size_z):
        total = total + in_z[(z + shift) % size_z].astype(f32)
    out_last[pl.ds(size_z, size_y)] = total
    for shift in shifts_y:
        to_y = (y + shift) % size_y
        send(out_last.at[size_z + to_y], in_last.at[y * size_c + core], sems_last, at(z, to_y, 1))
    theirs = (1 - core) * (size_z + y) + core * z
    send(
        out_last.at[theirs],
        in_last.at[(1 - core) * y * size_c + core * (z * size_c + 1)],
        sems_last,
        at(z, y, 1 - core),
    )
    mine = (1 - core) * z + core * (size_z + y)
    slot = (1 - core) * z * size_c + core * (y * size_c + 1)
    sources = size_z * size_c
    all_last = whole(out_last, in_last, sources - 1, sems_last)
    all_y.wait_send()
    all_z.wait_send()
    all_last.wait_recv()
    price = out_last[mine]
    for shift in range(1, sources):
        price = price + in_last[(slot + shift) % sources]
    price_ref[...] = price
    all_last.wait_send()


def finish(angles, price, cleared, angles_hbm, payment, sem):
    copy = pltpu.make_async_copy(angles, angles_hbm, sem)
    copy.start()
    payment[...] = cleared[...] * price[...]
    copy.wait()


def settle(torus, *operands):
    (
        kkt_inverse,
        demand,
        cost_quad,
        cost_lin,
        capacity,
        ramp,
        gen_start,
        boundary_bus,
        tie_count,
        part_bus,
        part_share,
        cleared_mw,
    ) = operands
    hours, buses = demand.shape
    tie_slots = boundary_bus.shape[2]
    parts, taps = part_share.shape
    pieces = parts // LANES
    size_z, size_y, size_c = torus
    chunks = max(1, buses // 256)
    line = lambda value: value.reshape(1, -1)
    vmem = pl.BlockSpec(memory_space=pltpu.VMEM)
    hbm = pl.BlockSpec(memory_space=pltpu.HBM)
    bf16, f32, i32 = jnp.bfloat16, jnp.float32, jnp.int32
    dma = pltpu.SemaphoreType.DMA
    angles, price = pl.pallas_call(
        functools.partial(kernel, torus),
        out_shape=(
            jax.ShapeDtypeStruct((hours, buses), f32),
            jax.ShapeDtypeStruct((pieces, LANES), f32),
        ),
        in_specs=[hbm] * 11,
        out_specs=(vmem, vmem),
        scratch_shapes=[
            pltpu.VMEM((2, tie_slots), i32),
            pltpu.VMEM((1, tie_count.shape[0]), i32),
            pltpu.VMEM((hours, buses), f32),
            pltpu.VMEM((buses, buses), bf16),
            pltpu.VMEM((1, buses), f32),
            pltpu.VMEM((1, buses), f32),
            pltpu.VMEM((1, buses), f32),
            pltpu.VMEM((1, buses), f32),
            pltpu.VMEM((1, buses), f32),
            pltpu.VMEM((taps, parts), i32),
            pltpu.VMEM((taps, parts), f32),
            pltpu.VMEM((hours, buses), bf16),
            pltpu.VMEM((hours, buses), bf16),
            pltpu.VMEM((hours, buses), f32),
            pltpu.VMEM((hours, buses), f32),
            pltpu.VMEM((PAD + hours, buses), f32),
            pltpu.VMEM((buses, 2 * tie_slots), bf16),
            pltpu.VMEM((taps * (buses // LANES), 16, LANES), bf16),
            pltpu.VMEM((buses, parts), bf16),
            pltpu.VMEM((2, hours, tie_slots), bf16),
            pltpu.VMEM((2, hours, tie_slots), bf16),
            pltpu.VMEM((1, buses), f32),
            pltpu.VMEM((1, buses), f32),
            pltpu.VMEM((hours * pieces, LANES), f32),
            pltpu.VMEM((size_y, size_z, pieces, LANES), bf16),
            pltpu.VMEM((size_z, size_y, pieces, LANES), bf16),
            pltpu.VMEM((size_y, size_z, pieces, LANES), bf16),
            pltpu.VMEM((size_z, size_y, pieces, LANES), bf16),
            pltpu.VMEM((size_z + size_y, pieces, LANES), f32),
            pltpu.VMEM((size_z * size_c, pieces, LANES), f32),
            dma((10,)),
            dma((chunks,)),
            dma((2,)),
            dma((2,)),
            dma((2,)),
            dma((2,)),
            dma((2,)),
            dma((2,)),
        ],
        compiler_params=pltpu.CompilerParams(
            collective_id=0, has_side_effects=True, vmem_limit_bytes=16 * 1024 * 1024
        ),
    )(*[pltpu.with_memory_space_constraint(v, pltpu.HBM) for v in (
        boundary_bus[0],
        line(tie_count),
        demand,
        kkt_inverse,
        line(cost_quad),
        line(cost_lin),
        line(capacity),
        line(ramp),
        line(gen_start),
        part_bus.T,
        part_share.T,
    )])
    angles, payment = pl.pallas_call(
        finish,
        out_shape=(
            jax.ShapeDtypeStruct((hours, buses), f32),
            jax.ShapeDtypeStruct((pieces, LANES), f32),
        ),
        in_specs=[vmem] * 3,
        out_specs=(pl.BlockSpec(memory_space=pl.ANY), vmem),
        scratch_shapes=[dma],
        compiler_params=pltpu.CompilerParams(vmem_limit_bytes=16 * 1024 * 1024),
    )(angles, price, cleared_mw.reshape(pieces, LANES))
    return angles, payment.reshape(cleared_mw.shape)


def solution(mesh, torus=(8, 8, 2)):
    return jax.shard_map(
        functools.partial(settle, torus),
        mesh=mesh,
        in_specs=(
            P("region", None, None),
            P("hour", "region"),
            P("region"),
            P("region"),
            P("region"),
            P("region"),
            P("region"),
            P("region", None, None),
            P(),
            P(),
            P(),
            P("hour", "region", None),
        ),
        out_specs=(P("hour", "region"), P("hour", "region", None)),
        check_vma=False,
    )
```

time: 39.1 us -> 32.6 us (0.83)
  Pallas kernels: 35 us -> 31.8 us
  local copies, waits for them, and re-layouts: 3.15 us -> 0.01 us
    pallas_call x1, Pallas kernels: 35 us -> 30.4 us  [settle(): pl.pallas_call(functools.partial(kernel, torus), out_shape=(jax.ShapeDtyp...]
    unnamed x2, local copies, waits for them, and re-layouts: 3.15 us -> 0.01 us
    pallas_call x0 -> x1, Pallas kernels: none -> 1.4 us  [settle(): pl.pallas_call(finish, out_shape=(jax.ShapeDtypeStruct((hours, buses), f3...]
where the time goes in v2:
time: 32.6 us; the launch traced here: 32.4 us
  Pallas kernels  31.8 us (98%)
  between operations  0.66 us (2%)
    pallas_call x1, Pallas kernels, settle(): pl.pallas_call(functools.partial(kernel, torus), out_shape=(jax.ShapeDtyp...  30.4 us
    pallas_call x1, Pallas kernels, settle(): pl.pallas_call(finish, out_shape=(jax.ShapeDtypeStruct((hours, buses), f3...  1.4 us

profile of v2, /device:TPU:1, one launch (start us, length us, event | category | flops | bytes accessed | tf_op | source)
XLA Modules:
  0.0 32.4 jit_solution(14115298220849549533)
XLA Ops:
  0.6 0.0 copy-start
  0.6 30.4 %shard_map.131 = (f32[128,1024]{1,0:T(8,128)S(1)}, f32[8,128]{1,0:T(8,128)S(1)}) custom-call(s32[2,128]{1,0:T(2,128)} %bitcast.19, s32[1,128]{1,0:T(1,128)} %bitcast.20, f32[128,1024]{1,0:T(8,128)} %demand_hbm.1, bf16[1,1024,1024]{2,1,0:T(8,128)(2,1)} %kkt_hbm.1, f32[1,1024]{1,0:T(1,128)} %bitcast.14, f32[1,1024]{1,0:T(1,128)} %bitcast.15, ...), custom_call_target="tpu_custom_call" | custom-call | tf_op jit(solution)/shard_map/pallas_call | solution.py:379
  31.0 0.0 copy-done
  31.1 1.4 %shard_map.132 = (f32[128,1024]{1,0:T(8,128)}, f32[8,128]{1,0:T(8,128)}) custom-call(f32[128,1024]{1,0:T(8,128)S(1)} %get-tuple-element.6.angles, f32[8,128]{1,0:T(8,128)S(1)} %get-tuple-element.7.price, f32[8,128]{1,0:T(8,128)S(1)} %bitcast.11), custom_call_target="tpu_custom_call" | custom-call | tf_op jit(solution)/shard_map/pallas_call | solution.py:443
Async XLA Ops:
  0.6 30.4 %copy-start = (f32[1,1,1024]{2,1,0:T(1,128)S(1)}, f32[1,1,1024]{2,1,0:T(1,128)}, u32[]{:S(2)}) copy-start(f32[1,1,1024]{2,1,0:T(1,128)} %param.23) | copy-start | bytes 12292

commit v3 on v2

--- a/solution.py
+++ b/solution.py
@@ -15,6 +15,13 @@
 
 def far_first(size):
     return sorted(range(1, size), key=lambda shift: -min(shift, size - shift))
+
+
+def far_first_all(torus):
+    size_z, size_y, _ = torus
+    shifts = [(a, b) for a in range(size_z) for b in range(size_y)]
+    hops = lambda shift: min(shift[0], size_z - shift[0]) + min(shift[1], size_y - shift[1])
+    return sorted(shifts[1:], key=lambda shift: -hops(shift))
 
 
 def kernel(
@@ -48,6 +55,9 @@
     base,
     dual,
     gen,
+    low_bound,
+    high_bound,
+    scale,
     slots,
     spread,
     shares,
@@ -56,20 +66,18 @@
     edge_out,
     edge_in,
     stage,
-    out_y,
-    out_z,
-    in_y,
-    in_z,
-    out_last,
-    in_last,
+    pair_out,
+    pair_in,
+    outbox,
+    inbox,
     load_sem,
     kkt_sem,
     tie_send,
     tie_recv,
     edge_sem,
-    ring_send,
-    ring_recv,
-    last_sem,
+    known,
+    pair_sem,
+    price_sem,
 ):
     size_z, size_y, size_c = torus
     regions = size_z * size_y * size_c
@@ -120,6 +128,7 @@
         )
         copy.start()
         kkt_loads.append(copy)
+    pair_of = min(2, chunks)
     cost_loads = [
         load(3, cost_quad_hbm, cost_quad),
         load(4, cost_lin_hbm, cost_lin),
@@ -167,17 +176,31 @@
 
     demand_load.wait()
     rhs[...] = demand[...].astype(bf16)
-    for c in range(chunks):
-        cols = pl.ds(c * chunk, chunk)
-        kkt_loads[c].wait()
-        angles = lax.dot_general(rhs[...], kkt[cols, :], NT, preferred_element_type=f32)
-        angles_ref[:, cols] = angles
-        part = jnp.dot(angles.astype(bf16), slots[cols, :], preferred_element_type=f32)
-        ends = part if c == 0 else ends + part
+    for first in range(0, chunks, pair_of):
+        for c in range(first, first + pair_of):
+            kkt_loads[c].wait()
+        both = [
+            lax.dot_general(
+                rhs[...], kkt[pl.ds(c * chunk, chunk), :], NT, preferred_element_type=f32
+            )
+            for c in range(first, first + pair_of)
+        ]
+        for c, angles in enumerate(both, first):
+            angles_ref[:, pl.ds(c * chunk, chunk)] = angles
+            part = jnp.dot(
+                angles.astype(bf16),
+                slots[pl.ds(c * chunk, chunk), :],
+                preferred_element_type=f32,
+            )
+            ends = part if c == 0 else ends + part
     for side in range(2):
         tie_out[side] = ends[:, side * tie_slots : (side + 1) * tie_slots].astype(bf16)
 
     pl.semaphore_wait(barrier, greeted)
+    for shift in shifts_y:
+        pl.semaphore_signal(
+            known, inc=1, device_id=at(z, (y + shift) % size_y, core), device_id_type=MESH
+        )
     ties = [
         send(tie_out.at[1 - side], tie_in.at[side], (tie_send.at[side], tie_recv.at[side]), to)
         for side, to in ((0, {"region": right}), (1, {"region": left}))
@@ -189,11 +212,11 @@
     start_row = (lax.broadcasted_iota(jnp.int32, (tall, chunk), 0) == 0) & (block == 0)
     for c in range(chunks):
         cols = pl.ds(c * chunk, chunk)
-        scale = 1.0 / (cost_quad[:, cols] + 1.0)
+        scale[:, cols] = 1.0 / (cost_quad[:, cols] + 1.0)
         for r in range(hours // tall):
             rows = pl.ds(r * tall, tall)
             angles = angles_ref[rows, cols]
-            target = (angles - cost_lin[:, cols]) * scale
+            target = (angles - cost_lin[:, cols]) * scale[:, cols]
             if r == 0:
                 prior = jnp.where(start_row, gen_start[:, cols], 0.0)
                 limited = jnp.minimum(
@@ -207,12 +230,19 @@
             dual[rows, cols] = owed
             base[rows, cols] = demand[rows, cols] + (made - owed)
         edge_out[:, cols] = made[tall - 1 :, :]
+        for r in range(hours // tall):
+            rows = pl.ds(r * tall, tall)
+            prior = gen[pl.ds(PAD - 1 + r * tall, tall), cols]
+            top = capacity[:, cols]
+            low_bound[rows, cols] = jnp.minimum(jnp.maximum(prior - ramp[:, cols], 0.0), top)
+            high_bound[rows, cols] = jnp.minimum(jnp.maximum(prior + ramp[:, cols], 0.0), top)
     edge = send(edge_out, edge_in, (edge_sem.at[0], edge_sem.at[1]), {"hour": later})
 
     for copy in part_loads:
         copy.wait()
     high = buses // LANES
-    tile = lax.broadcasted_iota(jnp.int32, (16, LANES), 0)
+    tile = lax.broadcasted_iota(jnp.int32, (16, LANES), 0).astype(f32).astype(bf16)
+    one, zero = jnp.ones((16, LANES), bf16), jnp.zeros((16, LANES), bf16)
 
     def fill(step, carry):
         cols = pl.ds(pl.multiple_of(step * LANES, LANES), LANES)
@@ -220,12 +250,14 @@
         for k in range(taps):
             local = part_bus[pl.ds(k, 1), cols] - region * buses
             share = part_share[pl.ds(k, 1), cols]
-            low.append(jnp.broadcast_to(local & (LANES - 1), (16, LANES)))
+            place = (local & (LANES - 1)).astype(f32)
+            low.append(jnp.broadcast_to(place, (16, LANES)).astype(bf16))
             for i in range(high):
                 held = jnp.where((local >> 7) == i, share, 0.0)
                 spread[k * high + i] = jnp.broadcast_to(held, (16, LANES)).astype(bf16)
         for t in range(LANES // 16):
-            ones = [jnp.where(tile + 16 * t == low[k], 1.0, 0.0).astype(bf16) for k in range(taps)]
+            place = tile + jnp.bfloat16(16 * t)
+            ones = [jnp.where(place == low[k], one, zero) for k in range(taps)]
             for i in range(high):
                 total = ones[0] * spread[i]
                 for k in range(1, taps):
@@ -250,24 +282,22 @@
         rhs[:, cols] = tied.astype(bf16)
 
     edge.wait()
-    gen[pl.ds(PAD - 1, 1), :] = jnp.where(block == 0, gen_start[...], edge_in[...])
+    prior = jnp.where(block == 0, gen_start[...], edge_in[...])
+    low_bound[pl.ds(0, 1), :] = jnp.minimum(jnp.maximum(prior - ramp[...], 0.0), capacity[...])
+    high_bound[pl.ds(0, 1), :] = jnp.minimum(jnp.maximum(prior + ramp[...], 0.0), capacity[...])
+    for first in range(0, chunks, pair_of):
+        for c in range(first, first + pair_of):
+            cols = pl.ds(c * chunk, chunk)
+            angles_ref[:, cols] = lax.dot_general(
+                rhs[...], kkt[cols, :], NT, preferred_element_type=f32
+            )
     for c in range(chunks):
         cols = pl.ds(c * chunk, chunk)
-        angles_ref[:, cols] = lax.dot_general(
-            rhs[...], kkt[cols, :], NT, preferred_element_type=f32
-        )
-    for c in range(chunks):
-        cols = pl.ds(c * chunk, chunk)
-        scale = 1.0 / (cost_quad[:, cols] + 1.0)
         for r in range(hours // tall):
             rows = pl.ds(r * tall, tall)
             owed = dual[rows, cols] + angles_ref[rows, cols]
-            prior = gen[pl.ds(PAD - 1 + r * tall, tall), cols]
-            target = (owed - cost_lin[:, cols]) * scale
-            limited = jnp.minimum(
-                jnp.maximum(target, prior - ramp[:, cols]), prior + ramp[:, cols]
-            )
-            made = jnp.minimum(jnp.maximum(limited, 0.0), capacity[:, cols])
+            target = (owed - cost_lin[:, cols]) * scale[:, cols]
+            made = jnp.minimum(jnp.maximum(target, low_bound[rows, cols]), high_bound[rows, cols])
             lmp[rows, cols] = (owed - made).astype(bf16)
 
     width = min(256, parts)
@@ -277,77 +307,58 @@
             stage[pl.ds(c * (width // LANES) + i, hours, stride=pieces), :] = part[
                 :, i * LANES : (i + 1) * LANES
             ]
-    for hour in range(hours):
-        to_z, to_y, to_c = hour // (size_y * size_c), (hour // size_c) % size_y, hour % size_c
-        row_price = stage[pl.ds(hour * pieces, pieces), :].astype(bf16)
-        if to_c == 0:
-            out_y[to_y, to_z] = row_price
-        else:
-            out_z[to_z, to_y] = row_price
-
-    sems_y = (ring_send.at[0], ring_recv.at[0])
-    sems_z = (ring_send.at[1], ring_recv.at[1])
-    for shift_y, shift_z in zip(shifts_y, shifts_z):
-        to_y, to_z = (y + shift_y) % size_y, (z + shift_z) % size_z
-        send(out_y.at[to_y], in_y.at[y], sems_y, at(z, to_y, core))
-        send(out_z.at[to_z], in_z.at[z], sems_z, at(to_z, y, core))
-
-    def whole(source, target, count, sems):
-        some = pl.ds(0, count)
-        return pltpu.make_async_remote_copy(
-            src_ref=source.at[some],
-            dst_ref=target.at[some],
-            send_sem=sems[0],
-            recv_sem=sems[1],
-            device_id={"region": right},
-            device_id_type=MESH,
+    chips = size_z * size_y
+
+    def priced(chip, owner):
+        return stage[pl.ds(pl.multiple_of((chip * size_c + owner) * pieces, pieces), pieces), :]
+
+    for chip in range(chips):
+        pair_out[chip] = priced(chip, 1 - core).astype(bf16)
+    pair = send(pair_out, pair_in, (pair_sem.at[0], pair_sem.at[1]), at(z, y, 1 - core))
+    to_zs = [(z + shift) % size_z * size_y for shift in range(size_z)]
+    to_ys = [(y + shift) % size_y for shift in range(size_y)]
+    pl.semaphore_wait(known, size_y - 1)
+    pair.wait()
+    for chip in range(chips):
+        outbox[chip] = (priced(chip, core) + pair_in[chip].astype(f32)).astype(bf16)
+
+    here = z * size_y + y
+    sems = (price_sem.at[0], price_sem.at[1])
+    for shift_z, shift_y in far_first_all(torus):
+        chip = to_zs[shift_z] + to_ys[shift_y]
+        send(outbox.at[chip], inbox.at[here], sems, {"region": chip * size_c + core})
+    inbox[here] = outbox[here]
+
+    others = pl.ds(0, chips - 1)
+    whole = pltpu.make_async_remote_copy(
+        src_ref=outbox.at[others],
+        dst_ref=inbox.at[others],
+        send_sem=sems[0],
+        recv_sem=sems[1],
+        device_id={"region": right},
+        device_id_type=MESH,
+    )
+    whole.wait_recv()
+    price_ref[...] = jnp.sum(inbox[...].astype(f32), axis=0)
+    whole.wait_send()
+
+
+def finish(angles, price, cleared, angles_hbm, payment_hbm, payment, sems):
+    rows = angles.shape[0] // 8
+    copies = [
+        pltpu.make_async_copy(
+            angles.at[pl.ds(i * rows, rows)], angles_hbm.at[pl.ds(i * rows, rows)], sems.at[i]
         )
-
-    all_y = whole(out_y, in_y, size_y - 1, sems_y)
-    all_z = whole(out_z, in_z, size_z - 1, sems_z)
-    all_y.wait_recv()
-    total = out_y[y].astype(f32)
-    for shift in range(1, size_y):
-        total = total + in_y[(y + shift) % size_y].astype(f32)
-    out_last[pl.ds(0, size_z)] = total
-    sems_last = (last_sem.at[0], last_sem.at[1])
-    for shift in shifts_z:
-        to_z = (z + shift) % size_z
-        send(out_last.at[to_z], in_last.at[z * size_c + core], sems_last, at(to_z, y, 0))
-    all_z.wait_recv()
-    total = out_z[z].astype(f32)
-    for shift in range(1, size_z):
-        total = total + in_z[(z + shift) % size_z].astype(f32)
-    out_last[pl.ds(size_z, size_y)] = total
-    for shift in shifts_y:
-        to_y = (y + shift) % size_y
-        send(out_last.at[size_z + to_y], in_last.at[y * size_c + core], sems_last, at(z, to_y, 1))
-    theirs = (1 - core) * (size_z + y) + core * z
-    send(
-        out_last.at[theirs],
-        in_last.at[(1 - core) * y * size_c + core * (z * size_c + 1)],
-        sems_last,
-        at(z, y, 1 - core),
-    )
-    mine = (1 - core) * z + core * (size_z + y)
-    slot = (1 - core) * z * size_c + core * (y * size_c + 1)
-    sources = size_z * size_c
-    all_last = whole(out_last, in_last, sources - 1, sems_last)
-    all_y.wait_send()
-    all_z.wait_send()
-    all_last.wait_recv()
-    price = out_last[mine]
-    for shift in range(1, sources):
-        price = price + in_last[(slot + shift) % sources]
-    price_ref[...] = price
-    all_last.wait_send()
-
-
-def finish(angles, price, cleared, angles_hbm, payment, sem):
-    copy = pltpu.make_async_copy(angles, angles_hbm, sem)
-    copy.start()
+        for i in range(8)
+    ]
+    for copy in copies:
+        copy.start()
     payment[...] = cleared[...] * price[...]
-    copy.wait()
+    last = pltpu.make_async_copy(payment, payment_hbm, sems.at[8])
+    last.start()
+    for copy in copies:
+        copy.wait()
+    last.wait()
 
 
 def settle(torus, *operands):
@@ -401,6 +412,9 @@
             pltpu.VMEM((hours, buses), f32),
             pltpu.VMEM((hours, buses), f32),
             pltpu.VMEM((PAD + hours, buses), f32),
+            pltpu.VMEM((hours, buses), f32),
+            pltpu.VMEM((hours, buses), f32),
+            pltpu.VMEM((1, buses), f32),
             pltpu.VMEM((buses, 2 * tie_slots), bf16),
             pltpu.VMEM((taps * (buses // LANES), 16, LANES), bf16),
             pltpu.VMEM((buses, parts), bf16),
@@ -409,18 +423,16 @@
             pltpu.VMEM((1, buses), f32),
             pltpu.VMEM((1, buses), f32),
             pltpu.VMEM((hours * pieces, LANES), f32),
-            pltpu.VMEM((size_y, size_z, pieces, LANES), bf16),
-            pltpu.VMEM((size_z, size_y, pieces, LANES), bf16),
-            pltpu.VMEM((size_y, size_z, pieces, LANES), bf16),
-            pltpu.VMEM((size_z, size_y, pieces, LANES), bf16),
-            pltpu.VMEM((size_z + size_y, pieces, LANES), f32),
-            pltpu.VMEM((size_z * size_c, pieces, LANES), f32),
+            pltpu.VMEM((size_z * size_y, pieces, LANES), bf16),
+            pltpu.VMEM((size_z * size_y, pieces, LANES), bf16),
+            pltpu.VMEM((size_z * size_y, pieces, LANES), bf16),
+            pltpu.VMEM((size_z * size_y, pieces, LANES), bf16),
             dma((10,)),
             dma((chunks,)),
             dma((2,)),
             dma((2,)),
             dma((2,)),
-            dma((2,)),
+            pltpu.SemaphoreType.REGULAR,
             dma((2,)),
             dma((2,)),
         ],
@@ -447,8 +459,8 @@
             jax.ShapeDtypeStruct((pieces, LANES), f32),
         ),
         in_specs=[vmem] * 3,
-        out_specs=(pl.BlockSpec(memory_space=pl.ANY), vmem),
-        scratch_shapes=[dma],
+        out_specs=(hbm, hbm),
+        scratch_shapes=[pltpu.VMEM((pieces, LANES), f32), dma((9,))],
         compiler_params=pltpu.CompilerParams(vmem_limit_bytes=16 * 1024 * 1024),
     )(angles, price, cleared_mw.reshape(pieces, LANES))
     return angles, payment.reshape(cleared_mw.shape)

time: 32.6 us -> 30 us (0.920)
  Pallas kernels: 31.8 us -> 29.2 us
    pallas_call x1, Pallas kernels: 30.4 us -> 28.4 us  [settle(): pl.pallas_call(functools.partial(kernel, torus), out_shape=(jax.ShapeDtyp...]
    pallas_call x1, Pallas kernels: 1.4 us -> 0.86 us  [settle(): pl.pallas_call(finish, out_shape=(jax.ShapeDtypeStruct((hours, buses), f3...]
where the time goes in v3:
time: 30 us; the launch traced here: 29.9 us
  Pallas kernels  29.2 us (97%)
  between operations  0.66 us (2%)
    pallas_call x1, Pallas kernels, settle(): pl.pallas_call(functools.partial(kernel, torus), out_shape=(jax.ShapeDtyp...  28.4 us
    pallas_call x1, Pallas kernels, settle(): pl.pallas_call(finish, out_shape=(jax.ShapeDtypeStruct((hours, buses), f3...  0.86 us

profile of v3, /device:TPU:1, one launch (start us, length us, event | category | flops | bytes accessed | tf_op | source)
XLA Modules:
  0.0 29.9 jit_solution(796270842532981678)
XLA Ops:
  0.6 0.0 copy-start
  0.6 28.4 %shard_map.131 = (f32[128,1024]{1,0:T(8,128)S(1)}, f32[8,128]{1,0:T(8,128)S(1)}) custom-call(s32[2,128]{1,0:T(2,128)} %bitcast.19, s32[1,128]{1,0:T(1,128)} %bitcast.20, f32[128,1024]{1,0:T(8,128)} %demand_hbm.1, bf16[1,1024,1024]{2,1,0:T(8,128)(2,1)} %kkt_hbm.1, f32[1,1024]{1,0:T(1,128)} %bitcast.14, f32[1,1024]{1,0:T(1,128)} %bitcast.15, ...), custom_call_target="tpu_custom_call" | custom-call | tf_op jit(solution)/shard_map/pallas_call | solution.py:390
  29.0 0.0 copy-done
  29.0 0.9 %shard_map.132 = (f32[128,1024]{1,0:T(8,128)}, f32[8,128]{1,0:T(8,128)}) custom-call(f32[128,1024]{1,0:T(8,128)S(1)} %get-tuple-element.6.angles, f32[8,128]{1,0:T(8,128)S(1)} %get-tuple-element.7.price, f32[8,128]{1,0:T(8,128)S(1)} %bitcast.11), custom_call_target="tpu_custom_call" | custom-call | tf_op jit(solution)/shard_map/pallas_call | solution.py:455
Async XLA Ops:
  0.6 28.4 %copy-start = (f32[1,1,1024]{2,1,0:T(1,128)S(1)}, f32[1,1,1024]{2,1,0:T(1,128)}, u32[]{:S(2)}) copy-start(f32[1,1,1024]{2,1,0:T(1,128)} %param.23) | copy-start | bytes 12292

commit v4 on v3

--- a/solution.py
+++ b/solution.py
@@ -11,6 +11,7 @@
 NT = (((1,), (1,)), ((), ()))
 LANES = 128
 PAD = 8
+GROUPS = 4
 
 
 def far_first(size):
@@ -138,26 +139,23 @@
     ]
     part_loads = [load(8, part_bus_hbm, part_bus), load(9, part_share_hbm, part_share)]
 
+    def along(step):
+        ys = sorted({step % size_y, -step % size_y} - {0})
+        zs = sorted({step % size_z, -step % size_z} - {0})
+        return [at(z, (y + shift) % size_y, core) for shift in ys] + [
+            at((z + shift) % size_z, y, core) for shift in zs
+        ]
+
+    def tell(sem, targets):
+        for target in targets:
+            pl.semaphore_signal(sem, inc=1, device_id=target, device_id_type=MESH)
+        return len(targets)
+
     barrier = pltpu.get_barrier_semaphore()
-    shifts_y = far_first(size_y)
-    shifts_z = far_first(size_z)
-    greeted = 0
-
-    def greet(to):
-        pl.semaphore_signal(barrier, inc=1, device_id=to, device_id_type=MESH)
-        return 1
-
-    for shift in shifts_y:
-        for other in range(size_c):
-            greeted += greet(at(z, (y + shift) % size_y, (core + other) % size_c))
-    for shift in shifts_z:
-        for other in range(size_c):
-            greeted += greet(at((z + shift) % size_z, y, (core + other) % size_c))
-    greeted += greet(at(z, y, 1 - core))
-    for neighbour in (right, left):
-        greeted += greet({"region": neighbour})
-    for neighbour in (earlier, later):
-        greeted += greet({"hour": neighbour})
+    near = along(1) + [{"region": right}, {"region": left}]
+    if blocks > 1:
+        near = near + [{"hour": earlier}, {"hour": later}]
+    greeted = tell(barrier, near)
 
     for copy in slot_loads:
         copy.wait()
@@ -173,6 +171,9 @@
             slots[pl.ds(c * chunk, chunk), pl.ds(side * tie_slots, tie_slots)] = jnp.where(
                 row + c * chunk == bus, 1.0, 0.0
             ).astype(bf16)
+
+    pl.semaphore_wait(barrier, greeted)
+    told = tell(known.at[0], along(1))
 
     demand_load.wait()
     rhs[...] = demand[...].astype(bf16)
@@ -196,15 +197,13 @@
     for side in range(2):
         tie_out[side] = ends[:, side * tie_slots : (side + 1) * tie_slots].astype(bf16)
 
-    pl.semaphore_wait(barrier, greeted)
-    for shift in shifts_y:
-        pl.semaphore_signal(
-            known, inc=1, device_id=at(z, (y + shift) % size_y, core), device_id_type=MESH
-        )
     ties = [
         send(tie_out.at[1 - side], tie_in.at[side], (tie_send.at[side], tie_recv.at[side]), to)
         for side, to in ((0, {"region": right}), (1, {"region": left}))
     ]
+
+    pl.semaphore_wait(known.at[0], told)
+    told = tell(known.at[1], along(2))
 
     for copy in cost_loads:
         copy.wait()
@@ -236,7 +235,8 @@
             top = capacity[:, cols]
             low_bound[rows, cols] = jnp.minimum(jnp.maximum(prior - ramp[:, cols], 0.0), top)
             high_bound[rows, cols] = jnp.minimum(jnp.maximum(prior + ramp[:, cols], 0.0), top)
-    edge = send(edge_out, edge_in, (edge_sem.at[0], edge_sem.at[1]), {"hour": later})
+    if blocks > 1:
+        edge = send(edge_out, edge_in, (edge_sem.at[0], edge_sem.at[1]), {"hour": later})
 
     for copy in part_loads:
         copy.wait()
@@ -265,7 +265,13 @@
                 shares[pl.ds(i * LANES + t * 16, 16), cols] = total
         return carry
 
-    lax.fori_loop(0, pieces, fill, 0)
+    early = pieces * 8 // 8
+    lax.fori_loop(0, early, fill, 0)
+    if told:
+        pl.semaphore_wait(known.at[1], told)
+    row_peers = [at(z, (y + shift) % size_y, core) for shift in far_first(size_y)]
+    told = tell(known.at[2], row_peers)
+    lax.fori_loop(early, pieces, fill, 0)
 
     for copy in ties:
         copy.wait()
@@ -281,8 +287,10 @@
             )
         rhs[:, cols] = tied.astype(bf16)
 
-    edge.wait()
-    prior = jnp.where(block == 0, gen_start[...], edge_in[...])
+    prior = gen_start[...]
+    if blocks > 1:
+        edge.wait()
+        prior = jnp.where(block == 0, prior, edge_in[...])
     low_bound[pl.ds(0, 1), :] = jnp.minimum(jnp.maximum(prior - ramp[...], 0.0), capacity[...])
     high_bound[pl.ds(0, 1), :] = jnp.minimum(jnp.maximum(prior + ramp[...], 0.0), capacity[...])
     for first in range(0, chunks, pair_of):
@@ -312,22 +320,42 @@
     def priced(chip, owner):
         return stage[pl.ds(pl.multiple_of((chip * size_c + owner) * pieces, pieces), pieces), :]
 
-    for chip in range(chips):
-        pair_out[chip] = priced(chip, 1 - core).astype(bf16)
-    pair = send(pair_out, pair_in, (pair_sem.at[0], pair_sem.at[1]), at(z, y, 1 - core))
+    here = z * size_y + y
     to_zs = [(z + shift) % size_z * size_y for shift in range(size_z)]
     to_ys = [(y + shift) % size_y for shift in range(size_y)]
-    pl.semaphore_wait(known, size_y - 1)
-    pair.wait()
-    for chip in range(chips):
-        outbox[chip] = (priced(chip, core) + pair_in[chip].astype(f32)).astype(bf16)
-
-    here = z * size_y + y
+    targets = [to_zs[shift_z] + to_ys[shift_y] for shift_z, shift_y in far_first_all(torus)]
+    farthest = targets[0]
+    targets = [jnp.where(here == 0, farthest, 0)] + [
+        jnp.where(chip == 0, farthest, chip) for chip in targets[1:]
+    ]
+    targets.append(here)
+    group = max(1, chips // GROUPS)
+    pairs = []
+    for start in range(0, chips, group):
+        for index in range(start, start + group):
+            pair_out[index] = priced(targets[index], 1 - core).astype(bf16)
+        some = pl.ds(start, group)
+        pairs.append(
+            send(
+                pair_out.at[some],
+                pair_in.at[some],
+                (pair_sem.at[0, start // group], pair_sem.at[1, start // group]),
+                at(z, y, 1 - core),
+            )
+        )
+    pl.semaphore_wait(known.at[2], told)
     sems = (price_sem.at[0], price_sem.at[1])
-    for shift_z, shift_y in far_first_all(torus):
-        chip = to_zs[shift_z] + to_ys[shift_y]
-        send(outbox.at[chip], inbox.at[here], sems, {"region": chip * size_c + core})
-    inbox[here] = outbox[here]
+    for start in range(0, chips, group):
+        pairs[start // group].wait_recv()
+        for index in range(start, start + group):
+            mixed = priced(targets[index], core) + pair_in[index].astype(f32)
+            outbox[index] = mixed.astype(bf16)
+        for index in range(start, min(start + group, chips - 1)):
+            to = {"region": targets[index] * size_c + core}
+            send(outbox.at[index], inbox.at[here], sems, to)
+    inbox[here] = outbox[chips - 1]
+    for pair in pairs:
+        pair.wait_send()
 
     others = pl.ds(0, chips - 1)
     whole = pltpu.make_async_remote_copy(
@@ -432,8 +460,8 @@
             dma((2,)),
             dma((2,)),
             dma((2,)),
-            pltpu.SemaphoreType.REGULAR,
-            dma((2,)),
+            pltpu.SemaphoreType.REGULAR((3,)),
+            dma((2, GROUPS)),
             dma((2,)),
         ],
         compiler_params=pltpu.CompilerParams(

time: 30 us -> 29.5 us (0.983)
  Pallas kernels: 29.2 us -> 28.7 us
    pallas_call x1, Pallas kernels: 28.4 us -> 27.9 us  [settle(): pl.pallas_call(functools.partial(kernel, torus), out_shape=(jax.ShapeDtyp...]
where the time goes in v4:
time: 29.5 us; the launch traced here: 29.4 us
  Pallas kernels  28.7 us (97%)
  between operations  0.66 us (2%)
    pallas_call x1, Pallas kernels, settle(): pl.pallas_call(functools.partial(kernel, torus), out_shape=(jax.ShapeDtyp...  27.9 us
    pallas_call x1, Pallas kernels, settle(): pl.pallas_call(finish, out_shape=(jax.ShapeDtypeStruct((hours, buses), f3...  0.86 us

profile of v4, /device:TPU:1, one launch (start us, length us, event | category | flops | bytes accessed | tf_op | source)
XLA Modules:
  0.0 29.4 jit_solution(16353620137305706267)
XLA Ops:
  0.6 0.0 copy-start
  0.6 27.9 %shard_map.131 = (f32[128,1024]{1,0:T(8,128)S(1)}, f32[8,128]{1,0:T(8,128)S(1)}) custom-call(s32[2,128]{1,0:T(2,128)} %bitcast.19, s32[1,128]{1,0:T(1,128)} %bitcast.20, f32[128,1024]{1,0:T(8,128)} %demand_hbm.1, bf16[1,1024,1024]{2,1,0:T(8,128)(2,1)} %kkt_hbm.1, f32[1,1024]{1,0:T(1,128)} %bitcast.14, f32[1,1024]{1,0:T(1,128)} %bitcast.15, ...), custom_call_target="tpu_custom_call" | custom-call | tf_op jit(solution)/shard_map/pallas_call | solution.py:418
  28.5 0.0 copy-done
  28.5 0.9 %shard_map.132 = (f32[128,1024]{1,0:T(8,128)}, f32[8,128]{1,0:T(8,128)}) custom-call(f32[128,1024]{1,0:T(8,128)S(1)} %get-tuple-element.6.angles, f32[8,128]{1,0:T(8,128)S(1)} %get-tuple-element.7.price, f32[8,128]{1,0:T(8,128)S(1)} %bitcast.11), custom_call_target="tpu_custom_call" | custom-call | tf_op jit(solution)/shard_map/pallas_call | solution.py:483
Async XLA Ops:
  0.6 27.9 %copy-start = (f32[1,1,1024]{2,1,0:T(1,128)S(1)}, f32[1,1,1024]{2,1,0:T(1,128)}, u32[]{:S(2)}) copy-start(f32[1,1,1024]{2,1,0:T(1,128)} %param.23) | copy-start | bytes 12292

commit v5 on v4

--- a/solution.py
+++ b/solution.py
@@ -202,9 +202,6 @@
         for side, to in ((0, {"region": right}), (1, {"region": left}))
     ]
 
-    pl.semaphore_wait(known.at[0], told)
-    told = tell(known.at[1], along(2))
-
     for copy in cost_loads:
         copy.wait()
     tall = min(32, hours)
@@ -237,6 +234,9 @@
             high_bound[rows, cols] = jnp.minimum(jnp.maximum(prior + ramp[:, cols], 0.0), top)
     if blocks > 1:
         edge = send(edge_out, edge_in, (edge_sem.at[0], edge_sem.at[1]), {"hour": later})
+
+    pl.semaphore_wait(known.at[0], told)
+    told = tell(known.at[1], along(2))
 
     for copy in part_loads:
         copy.wait()

time: 29.5 us -> 29.1 us (0.986)
  Pallas kernels: 28.7 us -> 28.3 us
    pallas_call x1, Pallas kernels: 27.9 us -> 27.4 us  [settle(): pl.pallas_call(functools.partial(kernel, torus), out_shape=(jax.ShapeDtyp...]
where the time goes in v5:
time: 29.1 us; the launch traced here: 29 us
  Pallas kernels  28.3 us (97%)
  between operations  0.66 us (2%)
    pallas_call x1, Pallas kernels, settle(): pl.pallas_call(functools.partial(kernel, torus), out_shape=(jax.ShapeDtyp...  27.4 us
    pallas_call x1, Pallas kernels, settle(): pl.pallas_call(finish, out_shape=(jax.ShapeDtypeStruct((hours, buses), f3...  0.86 us

profile of v5, /device:TPU:1, one launch (start us, length us, event | category | flops | bytes accessed | tf_op | source)
XLA Modules:
  0.0 29.0 jit_solution(1119267626167217274)
XLA Ops:
  0.6 0.0 copy-start
  0.6 27.4 %shard_map.131 = (f32[128,1024]{1,0:T(8,128)S(1)}, f32[8,128]{1,0:T(8,128)S(1)}) custom-call(s32[2,128]{1,0:T(2,128)} %bitcast.19, s32[1,128]{1,0:T(1,128)} %bitcast.20, f32[128,1024]{1,0:T(8,128)} %demand_hbm.1, bf16[1,1024,1024]{2,1,0:T(8,128)(2,1)} %kkt_hbm.1, f32[1,1024]{1,0:T(1,128)} %bitcast.14, f32[1,1024]{1,0:T(1,128)} %bitcast.15, ...), custom_call_target="tpu_custom_call" | custom-call | tf_op jit(solution)/shard_map/pallas_call | solution.py:418
  28.1 0.0 copy-done
  28.1 0.9 %shard_map.132 = (f32[128,1024]{1,0:T(8,128)}, f32[8,128]{1,0:T(8,128)}) custom-call(f32[128,1024]{1,0:T(8,128)S(1)} %get-tuple-element.6.angles, f32[8,128]{1,0:T(8,128)S(1)} %get-tuple-element.7.price, f32[8,128]{1,0:T(8,128)S(1)} %bitcast.11), custom_call_target="tpu_custom_call" | custom-call | tf_op jit(solution)/shard_map/pallas_call | solution.py:483
Async XLA Ops:
  0.6 27.5 %copy-start = (f32[1,1,1024]{2,1,0:T(1,128)S(1)}, f32[1,1,1024]{2,1,0:T(1,128)}, u32[]{:S(2)}) copy-start(f32[1,1,1024]{2,1,0:T(1,128)} %param.23) | copy-start | bytes 12292
